TPU v7x, 32 devices: a whole 2x2x4 slice. The times are simulated.
32 devices in a mesh: nodes: 16 (over z, y, x), stream: 2 (over core).
Axes of the slice: x: 2, y: 2, z: 4, core: 2. Of those that a mesh axis runs over, the one named last changes fastest.
Arguments:
- features: bfloat16 [5120, 1024], P('nodes'), may hold values from -6 to 6
- neighbours: int32 [5120, 50], P('nodes', 'stream'), may hold values from 0 to 5119, as said below
- present: int32 [5120, 50], P('nodes', 'stream'), may hold values from 0 to 1, as said below
- importance: int32 [5120, 50], P('nodes', 'stream'), may hold values from 1 to 64
- q_weight: bfloat16 [1024, 1024], replicated, may hold values from -0.1875 to 0.1875
- q_bias: float32 [1024], replicated, may hold values from -3 to 3
- w_weight: bfloat16 [2048, 1024], P('stream'), may hold values from -0.1875 to 0.1875
- w_bias: float32 [1024], replicated, may hold values from -3 to 3
- cotangent: bfloat16 [5120, 1024], P('nodes'), may hold values from -6 to 6
Outputs:
- embeddings: float32 [5120, 1024], P('nodes')
- feature_grad: float32 [5120, 1024], P('nodes', 'stream')
- q_weight_grad: float32 [1024, 1024], replicated
- q_bias_grad: float32 [1024], replicated
- w_weight_grad: float32 [2048, 1024], P('stream')
- w_bias_grad: float32 [1024], replicated
Inputs may be any that keep to these rules, and one draw needn't show every extreme that they name: `neighbours`: number a device's nodes' slots of one half of the 50 slots node by node, j = local node * 25 + slot within the half; slot j names a row of the block of 320 rows of device j % 16 of nodes, so that each device's block is named exactly 500 times by each device and half; a row may be named several times. Each node has between 5 and 50 present slots.
All inputs are finite; a program needn't handle non-finite values.
Results may differ from a plain program's by a relative error of at most 0.014.
The roundings to bfloat16 on the way count: a program that leaves them out, or rounds other values in their place, can miss the bound.
Values may be sent and summed in bfloat16 or wider, within the bound.
No kernel may reach another device: no remote copies, remote signals or barrier semaphores. Data moves between devices by JAX's collectives and lax.ppermute only.
A program may use at most 128 MiB of HBM per device.

v0:
```python
import jax
import jax.numpy as jnp
from jax import lax
from jax.sharding import PartitionSpec as P


def spread(value, axis, source):
    kept = jnp.where(lax.axis_index(axis) == source, value, 0).astype(value.dtype)
    return lax.psum(kept, axis)


def one_hot_rows(row_ids, count):
    return (row_ids[..., None] == jnp.arange(count, dtype=jnp.int32)).astype(jnp.bfloat16)


def on_device(
    features, neighbours, present, importance, q_weight, q_bias, w_weight, w_bias, cotangent
):
    node_rows, feature_dim = features.shape
    slot_count = neighbours.shape[1]
    owners_count = lax.axis_size("nodes")
    stream_index = lax.axis_index("stream")
    slot_total = node_rows * slot_count
    capacity = slot_total // owners_count
    local_row = neighbours.reshape(slot_total) % node_rows
    requests = local_row.reshape(capacity, owners_count).T
    shard_rows = lax.all_gather(features, "nodes", axis=0, tiled=True)
    shards = shard_rows.shape[0] // node_rows
    blocks_of = shard_rows.reshape(shards, node_rows, feature_dim)
    picked = jnp.einsum(
        "scr,srd->scd",
        one_hot_rows(requests, node_rows),
        blocks_of,
        preferred_element_type=jnp.float32,
    ).astype(jnp.bfloat16)
    slot_rows = jnp.transpose(picked, (1, 0, 2)).reshape(slot_total, feature_dim)
    weights = (present * importance).astype(jnp.float32)
    weight_half = jnp.sum(weights, axis=1)
    block_nodes = 32
    steps_count = node_rows // block_nodes
    row_blocks = slot_rows.reshape(steps_count, block_nodes * slot_count, feature_dim)
    weight_blocks = weights.reshape(steps_count, block_nodes, slot_count)

    def hidden_of(collected_rows):
        return jnp.dot(collected_rows, q_weight, preferred_element_type=jnp.float32) + q_bias

    def forward_block(inputs):
        collected_rows, importance_block_weights = inputs
        hidden_pre = hidden_of(collected_rows)
        hidden_state = jax.nn.relu(hidden_pre).reshape(block_nodes, slot_count, feature_dim)
        return jnp.einsum(
            "gk,gkd->gd", importance_block_weights, hidden_state, precision=lax.Precision.HIGHEST
        )

    weighted_numerator = lax.map(forward_block, (row_blocks, weight_blocks)).reshape(
        node_rows, feature_dim
    )
    weighted_numerator, weight_sum = lax.psum((weighted_numerator, weight_half), "stream")
    aggregate = (weighted_numerator / weight_sum[:, None]).astype(jnp.bfloat16)
    stream_input = jnp.where(stream_index == 0, features, aggregate)
    partial_value = jnp.dot(stream_input, w_weight, preferred_element_type=jnp.float32)
    linear = lax.psum(partial_value, "stream") + w_bias
    relu_out = jax.nn.relu(linear)
    norm_scale = lax.rsqrt(jnp.mean(relu_out * relu_out, axis=1, keepdims=True) + 1e-06)
    embeddings = relu_out * norm_scale
    grad_out = cotangent.astype(jnp.float32)
    grad_relu = norm_scale * grad_out - relu_out * (
        norm_scale * norm_scale * norm_scale
    ) * jnp.mean(relu_out * grad_out, axis=1, keepdims=True)
    grad_linear = jnp.where(linear > 0, grad_relu, 0.0).astype(jnp.bfloat16)
    w_grad_local = lax.dot_general(
        stream_input, grad_linear, (((0,), (0,)), ((), ())), preferred_element_type=jnp.float32
    )
    w_bias_local = jnp.sum(grad_linear.astype(jnp.float32), axis=0)
    back_rows = lax.dot_general(
        grad_linear, w_weight, (((1,), (1,)), ((), ())), preferred_element_type=jnp.float32
    )
    grad_aggregate = spread(back_rows, "stream", 1)
    self_grad = jnp.where(stream_index == 0, back_rows, 0.0)
    grad_sum = grad_aggregate / weight_sum[:, None]
    grad_blocks = grad_sum.reshape(steps_count, block_nodes, feature_dim)

    def backward_block(totals, inputs):
        q_total, bias_total = totals
        collected_rows, importance_block_weights, grad_block = inputs
        hidden_pre = hidden_of(collected_rows)
        grad_hidden = (importance_block_weights[:, :, None] * grad_block[:, None, :]).reshape(
            block_nodes * slot_count, feature_dim
        )
        grad_hidden = jnp.where(hidden_pre > 0, grad_hidden, 0.0).astype(jnp.bfloat16)
        q_total = q_total + lax.dot_general(
            collected_rows,
            grad_hidden,
            (((0,), (0,)), ((), ())),
            preferred_element_type=jnp.float32,
        )
        bias_total = bias_total + jnp.sum(grad_hidden.astype(jnp.float32), axis=0)
        grad_rows = lax.dot_general(
            grad_hidden, q_weight, (((1,), (1,)), ((), ())), preferred_element_type=jnp.float32
        ).astype(jnp.bfloat16)
        return ((q_total, bias_total), grad_rows)

    start_totals = (
        jnp.zeros((feature_dim, feature_dim), jnp.float32),
        jnp.zeros((feature_dim,), jnp.float32),
    )
    (q_grad_local, q_bias_local), grad_rows = lax.scan(
        backward_block, start_totals, (row_blocks, weight_blocks, grad_blocks)
    )
    grad_buffer = jnp.transpose(grad_rows.reshape(capacity, owners_count, feature_dim), (1, 0, 2))
    asked_rows, returned = (
        lax.all_to_all(requests, "nodes", split_axis=0, concat_axis=0, tiled=True),
        lax.all_to_all(grad_buffer, "nodes", split_axis=0, concat_axis=0, tiled=True),
    )
    neighbour_grad = lax.dot_general(
        one_hot_rows(asked_rows.reshape(-1), node_rows),
        returned.reshape(-1, feature_dim),
        (((0,), (0,)), ((), ())),
        preferred_element_type=jnp.float32,
    )
    feature_grad = lax.psum_scatter(
        self_grad + neighbour_grad, "stream", scatter_dimension=1, tiled=True
    )
    w_grad, w_bias_grad, q_grad, q_bias_grad = lax.psum(
        (w_grad_local, w_bias_local, q_grad_local, q_bias_local), "nodes"
    )
    q_grad, q_bias_grad = lax.psum((q_grad, q_bias_grad), "stream")
    return (embeddings, feature_grad, q_grad, q_bias_grad, w_grad, w_bias_grad)


def solution(mesh):
    in_specs = (
        P("nodes", None),
        P("nodes", "stream"),
        P("nodes", "stream"),
        P("nodes", "stream"),
        P(),
        P(),
        P("stream", None),
        P(),
        P("nodes", None),
    )
    out_specs = (P("nodes", None), P("nodes", "stream"), P(), P(), P("stream", None), P())
    return jax.shard_map(
        on_device, mesh=mesh, in_specs=in_specs, out_specs=out_specs, check_vma=False
    )
```

profile of v0, /device:TPU:0, one launch (start us, length us, event | category | flops | bytes accessed | tf_op | source)
XLA Modules:
  0.0 1334.9 jit_solution(5990324770737478218)
XLA Ops:
  10.2 135.5 %all-gather.2.cloned.1.call-done = bf16[5120,1024]{1,0:T(8,128)(2,1)} async-done(((bf16[320,1024]{1,0:T(8,128)(2,1)}), bf16[5120,1024]{1,0:T(8,128)(2,1)}) %all-gather.2.cloned.1.call-update) | async-done | bytes 10485776 | tf_op jit(solution)/shard_map/all_gather | solution.py:27
  145.7 16.2 %convert_bitcast_fusion = bf16[500,16,1024]{2,0,1:T(8,128)(2,1)} fusion(bf16[16,320,1024]{2,1,0:T(8,128)(2,1)} %bitcast.85, s32[16,500]{1,0:T(8,128)S(1)} %copy.35), kind=kOutput, calls=%fused_computation.22 | convolution fusion | flops 5253632000 | bytes 26901760 | tf_op jit(solution)/shard_map/scr,srd->scd/dot_general | solution.py:30
  161.9 15.5 %copy.36 = bf16[500,16,1024]{2,1,0:T(8,128)(2,1)} copy(bf16[500,16,1024]{2,0,1:T(8,128)(2,1)} %convert_bitcast_fusion) | data formatting | bytes 32768000 | tf_op jit(solution)/shard_map/convert_element_type | solution.py:35
  177.4 143.1 %while.25 = (s32[]{:T(128)}, f32[10,32,1024]{2,1,0:T(8,128)}, f32[10,32,25]{2,1,0:T(8,128)S(1)}, bf16[10,800,1024]{2,1,0:T(8,128)(2,1)}, bf16[1024,1024]{1,0:T(8,128)(2,1)}, /*index=5*/f32[1024]{0:T(1024)S(1)}, s32[]{:T(128)}) while((s32[]{:T(128)}, f32[10,32,1024]{2,1,0:T(8,128)}, f32[10,32,25]{2,1,0:T(8,128)S(1)}, ...), condition=%wide.region_1.2_spmd, body=%wide.region_0.1_spmd.sunk | while | flops 1689190400 | bytes 17250768 | solution.py:55
  177.4 5.7 add_maximum_fusion.3
  183.2 3.7 reshape.83
  186.8 4.3 fusion.56
  191.8 5.7 add_maximum_fusion.3
  197.5 3.7 reshape.83
  201.1 4.3 fusion.56
  206.1 5.7 add_maximum_fusion.3
  211.8 3.7 reshape.83
  215.4 4.3 fusion.56
  220.4 5.7 add_maximum_fusion.3
  226.0 3.7 reshape.83
  229.7 4.3 fusion.56
  234.7 5.7 add_maximum_fusion.3
  240.3 3.7 reshape.83
  244.0 4.3 fusion.56
  249.0 5.7 add_maximum_fusion.3
  254.6 3.7 reshape.83
  258.3 4.3 fusion.56
  263.3 5.7 add_maximum_fusion.3
  272.6 4.3 fusion.56
  277.6 5.7 add_maximum_fusion.3
  283.2 3.7 reshape.83
  286.9 4.3 fusion.56
  291.9 5.7 add_maximum_fusion.3
  301.2 4.3 fusion.56
  306.2 5.7 add_maximum_fusion.3
  311.8 3.7 reshape.83
  315.5 4.3 fusion.56
  323.0 15.8 %all-reduce.8.cloned.1.call-done = f32[320,1024]{1,0:T(8,128)} async-done(((f32[320,1024]{1,0:T(8,128)}), f32[320,1024]{1,0:T(8,128)}) %all-reduce.8.cloned.1.call-update) | async-done | bytes 1310736 | tf_op jit(solution)/shard_map/psum | solution.py:58
  342.7 21.1 %all-reduce.10.cloned.1.call-done = f32[320,1024]{1,0:T(8,128)} async-done(((f32[320,1024]{1,0:T(8,128)}), f32[320,1024]{1,0:T(8,128)}) %all-reduce.10.cloned.1.call-update) | async-done | bytes 1310736 | tf_op jit(solution)/shard_map/psum | solution.py:62
  371.3 6.8 all-to-all-start
  378.1 12.8 all-reduce.12.cloned.1.call-done
  392.5 239.1 %while.26 = (s32[]{:T(128)}, f32[1024,1024]{1,0:T(8,128)}, f32[1024]{0:T(1024)S(1)}, bf16[10,800,1024]{2,1,0:T(8,128)(2,1)}, bf16[10,800,1024]{2,1,0:T(8,128)(2,...) while((s32[]{:T(128)}, f32[1024,1024]{1,0:T(8,128)}, ...), condition=%wide.region_11.12_spmd.clone, body=%wide.region_9.11_spmd.clone.sunk | while | flops 5041816576 | bytes 50894132 | solution.py:107
  399.4 5.2 convert_reduce_fusion.3
  408.9 6.3 select_add_fusion.4
  422.2 5.2 convert_reduce_fusion.3
  431.7 7.6 select_add_fusion.4
  446.2 5.2 convert_reduce_fusion.3
  455.7 7.6 select_add_fusion.4
  470.3 5.2 convert_reduce_fusion.3
  479.7 7.6 select_add_fusion.4
  494.3 5.2 convert_reduce_fusion.3
  503.7 7.6 select_add_fusion.4
  518.3 5.2 convert_reduce_fusion.3
  527.8 7.6 select_add_fusion.4
  542.4 5.2 convert_reduce_fusion.3
  551.9 7.6 select_add_fusion.4
  566.4 5.2 convert_reduce_fusion.3
  575.9 7.6 select_add_fusion.4
  590.4 5.2 convert_reduce_fusion.3
  599.9 7.6 select_add_fusion.4
  614.5 5.2 convert_reduce_fusion.3
  624.0 7.6 select_add_fusion.4
  631.6 15.5 %copy.43 = bf16[500,16,1024]{2,0,1:T(8,128)(2,1)} copy(bf16[500,16,1024]{2,1,0:T(8,128)(2,1)} %bitcast.14) | data formatting | bytes 32768000 | tf_op jit(solution)/shard_map/reshape | solution.py:110
  647.1 6.8 all-to-all-start.1
  657.3 592.5 %all-reduce.16.cloned.1.call-done = (f32[1024,1024]{1,0:T(8,128)}, f32[1024,1024]{1,0:T(8,128)}) async-done(((f32[1024,1024]{1,0:T(8,128)}, f32[1024,1024]{1,0:T(8,128)}), (f32[1024,1024]{1,0:T(8,128)}, f32[1024,1024]{1,0:T(8,128)})) %all-reduce.16.cloned.1.call-update) | async-done | bytes 8388624 | tf_op jit(solution)/shard_map/psum | solution.py:124
  1250.3 15.0 %reshape.78 = bf16[8000,1024]{1,0:T(8,128)(2,1)} reshape(bf16[16,500,1024]{2,1,0:T(8,128)(2,1)} %all-to-all-done.1) | data formatting | bytes 32768000 | tf_op jit(solution)/shard_map/reshape | solution.py:117
  1265.3 10.4 fusion.13
  1275.7 41.2 %all-reduce = (f32[1024]{0:T(1024)S(1)}, f32[1024]{0:T(1024)}) all-reduce(f32[1024]{0:T(1024)S(1)} %get-tuple-element.90, f32[1024]{0:T(1024)S(1)} %get-tuple-element.157), channel_id=1, replica_groups=mesh['nodes'=16,'stream'=2] {'nodes'}, use_global_device_ids=true, to_apply=%region_15.16 | all-reduce | flops 2048 | bytes 16384 | tf_op jit(solution)/shard_map/psum | solution.py:124
  1320.0 4.9 copy.72
  (201 shorter events, 154.5 us)
Async XLA Ops:
  7.2 333.3 %copy-start = (bf16[1024,1024]{1,0:T(8,128)(2,1)S(1)}, bf16[1024,1024]{1,0:T(8,128)(2,1)}, u32[]{:S(2)}) copy-start(bf16[1024,1024]{1,0:T(8,128)(2,1)} %param.19) | copy-start | bytes 6291460
  7.2 2.8 copy-start.9
  7.2 2.8 copy-start.10
  7.2 138.5 %all-gather.2.cloned.1.call-start = ((), (), s32[]{:S(2)}) async-start(), calls=%async_computation.3 | async-start | bytes 11141120 | tf_op jit(solution)/shard_map/all_gather | solution.py:27
  7.9 330.9 %all-reduce.8.cloned.1.call-start = ((), (), s32[]{:S(2)}) async-start(), calls=%async_computation.4 | async-start | bytes 2621440 | tf_op jit(solution)/shard_map/psum | solution.py:58
  161.9 15.5 %copy-start.13 = (f32[1024]{0:T(1024)S(1)}, f32[1024]{0:T(1024)}, u32[]{:S(2)}) copy-start(f32[1024]{0:T(1024)} %param.18) | copy-start | bytes 12292
  177.4 161.4 %copy-start.4 = (bf16[320,1024]{1,0:T(8,128)(2,1)S(1)}, bf16[320,1024]{1,0:T(8,128)(2,1)}, u32[]{:S(2)}) copy-start(bf16[320,1024]{1,0:T(8,128)(2,1)} %param.13) | copy-start | bytes 1966084
  320.5 2.6 copy-start.8
  320.5 43.2 %all-reduce.10.cloned.1.call-start = ((), (), s32[]{:S(2)}) async-start(), calls=%async_computation.5 | async-start | bytes 2621440 | tf_op jit(solution)/shard_map/psum | solution.py:62
  340.5 23.3 %copy-start.5 = (bf16[320,1024]{1,0:T(8,128)(2,1)S(1)}, bf16[320,1024]{1,0:T(8,128)(2,1)}, u32[]{:S(2)}) copy-start(bf16[320,1024]{1,0:T(8,128)(2,1)} %param.21) | copy-start | bytes 1966084
  340.5 23.3 %copy-start.11 = (f32[1024]{0:T(1024)S(1)}, f32[1024]{0:T(1024)}, u32[]{:S(2)}) copy-start(f32[1024]{0:T(1024)} %param.20) | copy-start | bytes 12292
  342.4 48.5 %all-reduce.12.cloned.1.call-start = ((), (), s32[]{:S(2)}) async-start(), calls=%async_computation.6 | async-start | bytes 2621440 | tf_op jit(solution)/shard_map/psum | solution.py:9
  363.8 1.9 copy-start.2
  363.8 1.9 copy-start.6
  371.3 275.8 %all-to-all-start = ((s32[16,1,500]{2,1,0:T(1,128)}), s32[16,1,500]{2,1,0:T(1,128)S(1)}, u32[]{:S(2)}, u32[]{:S(2)}) async-start(s32[16,1,500]{2,1,0:T(1,128)} %copy.37), calls=%async_computation | async-start | bytes 65536 | tf_op jit(solution)/shard_map/all_to_all | solution.py:112
  399.4 6.4 copy-start.12
  404.7 1.2 copy-start.14
  422.2 6.4 copy-start.12
  427.4 1.2 copy-start.14
  446.2 6.4 copy-start.12
  451.4 1.2 copy-start.14
  470.3 6.4 copy-start.12
  475.5 1.2 copy-start.14
  494.3 6.4 copy-start.12
  499.5 1.2 copy-start.14
  518.3 6.4 copy-start.12
  523.5 1.2 copy-start.14
  542.4 6.4 copy-start.12
  547.6 1.2 copy-start.14
  566.4 6.4 copy-start.12
  571.7 1.2 copy-start.14
  590.4 6.4 copy-start.12
  595.7 1.2 copy-start.14
  614.5 6.4 copy-start.12
  619.7 1.2 copy-start.14
  647.1 603.3 %all-to-all-start.1 = ((bf16[16,500,1024]{2,1,0:T(8,128)(2,1)}), bf16[16,500,1024]{2,1,0:T(8,128)(2,1)}, u32[]{:S(2)}, u32[]{:S(2)}) async-start(bf16[16,500,1024]{2,1,0:T(8,128)(2,1)} %bitcast.80), calls=%async_computation.1 | async-start | bytes 33030144 | tf_op jit(solution)/shard_map/all_to_all | solution.py:113
  653.9 595.9 %all-reduce.16.cloned.1.call-start = ((), (), s32[]{:S(2)}) async-start(), calls=%async_computation.9 | async-start | bytes 16777216 | tf_op jit(solution)/shard_map/psum | solution.py:124
  657.3 662.7 %all-reduce.14.cloned.1.call-start = ((), (), s32[]{:S(2)}) async-start(), calls=%async_computation.8 | async-start | bytes 8388608 | tf_op jit(solution)/shard_map/psum | solution.py:127
  1249.9 70.1 %reduce-scatter.2.cloned.1.call-start = ((), (), s32[]{:S(2)}) async-start(), calls=%async_computation.7 | async-start | bytes 1966080 | tf_op jit(solution)/shard_map/reduce_scatter | solution.py:121
  1250.3 15.0 %copy-start.7 = (f32[320,1024]{1,0:T(8,128)S(1)}, f32[320,1024]{1,0:T(8,128)}, u32[]{:S(2)}) copy-start(f32[320,1024]{1,0:T(8,128)} %get-tuple-element.169) | copy-start | bytes 3932164
  1320.0 4.9 copy-start.3
  1324.9 3.1 copy-start.1
Sparse Core Ops, SparseCore 0:
  10.7 134.8 all-gather.1
  320.6 18.1 all-reduce.7
  342.5 21.1 all-reduce.9
  369.8 21.1 all-reduce.11
  662.3 587.4 all-reduce.15
  1252.3 27.3 all-reduce.13
  1282.6 9.9 reduce-scatter.1
where the time goes:
time: 1340 us; the launch traced here: 1330 us
  waiting for transfers between devices  779 us (58%)
  matrix products  291 us (22%)
  local copies, waits for them, and re-layouts  181 us (14%)
  blocking collectives  46.7 us (3%)
  starting transfers between devices  14.3 us (1%)
  between operations  14.3 us (1%)
    psum x1, waiting for transfers between devices, on_device(): lax.psum((w_grad_local, w_bias_local, q_grad_local, q_bias_local), 'nodes')  593 us
    all_gather x1, waiting for transfers between devices, on_device(): shard_rows = lax.all_gather(features, 'nodes', axis=0, tiled=True)  135 us
    dot_general x20, matrix products, hidden_of(): jnp.dot(collected_rows, q_weight, preferred_element_type=jnp.float32)  109 us
    dot_general x10, matrix products, backward_block(): lax.dot_general(collected_rows, grad_hidden, (((0,), (0,)), ((), ())), pr...  74.6 us
    mul x40, local copies, waits for them, and re-layouts, backward_block(): importance_block_weights[:, :, None] * grad_block[:, None, :]  62.3 us
    dot_general x10, matrix products, forward_block(): jnp.einsum('gk,gkd->gd', importance_block_weights, hidden_state, precisio...  42.9 us
    psum x1, blocking collectives, on_device(): lax.psum((w_grad_local, w_bias_local, q_grad_local, q_bias_local), 'nodes')  41.2 us
    reshape x10, local copies, waits for them, and re-layouts, forward_block(): jax.nn.relu(hidden_pre).reshape(block_nodes, slot_count, feature_dim)  36.6 us
  transfers between devices with their start and end apart: 9, of which 5 were waited for; matrix products, arithmetic and copies ran while one was open for 21% of the time, Pallas kernels for 0%

commit v1 on v0

--- a/solution.py
+++ b/solution.py
@@ -2,6 +2,27 @@
 import jax.numpy as jnp
 from jax import lax
 from jax.sharding import PartitionSpec as P
+
+
+def collect(x, axis, dim):
+    size, mine, extent = (lax.axis_size(axis), lax.axis_index(axis), x.shape[dim])
+    right = [(i, (i + 1) % size) for i in range(size)]
+    downward = [(i, (i - 1) % size) for i in range(size)]
+    result = jnp.zeros((*x.shape[:dim], size * extent, *x.shape[dim + 1 :]), x.dtype)
+    result = lax.dynamic_update_slice_in_dim(result, x, mine * extent, axis=dim)
+    from_left = from_right = x
+    halfway = size // 2
+    for hop in range(1, halfway + 1):
+        from_left = lax.ppermute(from_left, axis, right)
+        result = lax.dynamic_update_slice_in_dim(
+            result, from_left, (mine - hop) % size * extent, axis=dim
+        )
+        if hop < size - halfway:
+            from_right = lax.ppermute(from_right, axis, downward)
+            result = lax.dynamic_update_slice_in_dim(
+                result, from_right, (mine + hop) % size * extent, axis=dim
+            )
+    return result
 
 
 def spread(value, axis, source):
@@ -24,7 +45,7 @@
     capacity = slot_total // owners_count
     local_row = neighbours.reshape(slot_total) % node_rows
     requests = local_row.reshape(capacity, owners_count).T
-    shard_rows = lax.all_gather(features, "nodes", axis=0, tiled=True)
+    shard_rows = collect(features, "nodes", 0)
     shards = shard_rows.shape[0] // node_rows
     blocks_of = shard_rows.reshape(shards, node_rows, feature_dim)
     picked = jnp.einsum(

time: 1340 us -> 1450 us (1.082)
  starting transfers between devices: 14.3 us -> 118 us
  local copies, waits for them, and re-layouts: 181 us -> 214 us
  waiting for transfers between devices: 779 us -> 749 us
    all_gather x1 -> x0, waiting for transfers between devices: 135 us -> none  [on_device(): shard_rows = lax.all_gather(features, 'nodes', axis=0, tiled=True)]
    ppermute x0 -> x15, starting transfers between devices: none -> 104 us  [the longest x7 90.6 us: collect(): from_right = lax.ppermute(from_right, axis, downward)]
    ppermute x0 -> x15, waiting for transfers between devices: none -> 99.4 us  [the longest x8 88.4 us: collect(): from_left = lax.ppermute(from_left, axis, right)]
    dynamic_update_slice x0 -> x16, local copies, waits for them, and re-layouts: none -> 20.8 us  [the longest x8 10.4 us: collect(): lax.dynamic_update_slice_in_dim(result, from_left, (mine - hop) % size *...]
  transfers between devices with their start and end apart: 9 -> 23, of which waited for: 5 -> 12; matrix products, arithmetic and copies ran while one was open for 21% -> 21% of each run, Pallas kernels for 0% -> 0%
where the time goes in v1:
time: 1450 us; the launch traced here: 1440 us
  waiting for transfers between devices  749 us (52%)
  matrix products  291 us (20%)
  local copies, waits for them, and re-layouts  214 us (15%)
  starting transfers between devices  118 us (8%)
  blocking collectives  46.8 us (3%)
    psum x1, waiting for transfers between devices, on_device(): lax.psum((w_grad_local, w_bias_local, q_grad_local, q_bias_local), 'nodes')  592 us
    dot_general x20, matrix products, hidden_of(): jnp.dot(collected_rows, q_weight, preferred_element_type=jnp.float32)  109 us
    ppermute x7, starting transfers between devices, collect(): from_right = lax.ppermute(from_right, axis, downward)  90.6 us
    ppermute x8, waiting for transfers between devices, collect(): from_left = lax.ppermute(from_left, axis, right)  88.4 us
    dot_general x10, matrix products, backward_block(): lax.dot_general(collected_rows, grad_hidden, (((0,), (0,)), ((), ())), pr...  74.6 us
    mul x40, local copies, waits for them, and re-layouts, backward_block(): importance_block_weights[:, :, None] * grad_block[:, None, :]  62.7 us
    dot_general x10, matrix products, forward_block(): jnp.einsum('gk,gkd->gd', importance_block_weights, hidden_state, precisio...  42.9 us
    psum x1, blocking collectives, on_device(): lax.psum((w_grad_local, w_bias_local, q_grad_local, q_bias_local), 'nodes')  41.3 us
  transfers between devices with their start and end apart: 23, of which 12 were waited for; matrix products, arithmetic and copies ran while one was open for 21% of the time, Pallas kernels for 0%

profile of v1, /device:TPU:0, one launch (start us, length us, event | category | flops | bytes accessed | tf_op | source)
XLA Modules:
  0.0 1444.3 jit_solution(4662037514169532764)
XLA Ops:
  14.3 24.3 %collective-permute-done = bf16[320,1024]{1,0:T(8,128)(2,1)S(1)} collective-permute-done((bf16[320,1024]{1,0:T(8,128)(2,1)}, bf16[320,1024]{1,0:T(8,128)(2,1)S(1)}, u32[]{:S(2)}, u32[]{:S(2)}) %collective-permute-start) | collective-permute-done | bytes 655392 | tf_op jit(solution)/shard_map/ppermute | solution.py:16
  44.2 23.9 %collective-permute-done.2 = bf16[320,1024]{1,0:T(8,128)(2,1)S(1)} collective-permute-done((bf16[320,1024]{1,0:T(8,128)(2,1)S(1)}, bf16[320,1024]{1,0:T(8,128)(2,1)S(1)}, u32[]{:S(2)}, u32[]{:S(2)}) %collective-permute-start.2) | collective-permute-done | bytes 655392 | tf_op jit(solution)/shard_map/ppermute | solution.py:16
  73.7 23.1 %collective-permute-done.4 = bf16[320,1024]{1,0:T(8,128)(2,1)S(1)} collective-permute-done((bf16[320,1024]{1,0:T(8,128)(2,1)S(1)}, bf16[320,1024]{1,0:T(8,128)(2,1)S(1)}, u32[]{:S(2)}, u32[]{:S(2)}) %collective-permute-start.4) | collective-permute-done | bytes 655392 | tf_op jit(solution)/shard_map/ppermute | solution.py:16
  99.3 16.0 %collective-permute-start.7 = (bf16[320,1024]{1,0:T(8,128)(2,1)}, bf16[320,1024]{1,0:T(8,128)(2,1)}, u32[]{:S(2)}, u32[]{:S(2)}) collective-permute-start(bf16[320,1024]{1,0:T(8,128)(2,1)} %collective-permute-done.5), channel_id=1, source_target_pairs={{0,30},{2,0},{4,2},{6,4},{8,6},{10,8},{12,10},{14,12},{16,14},{18,... | collective-permute-start | bytes 1966088 | tf_op jit(solution)/shard_map/ppermute | solution.py:21
  115.3 10.2 collective-permute-done.6
  129.3 31.2 %collective-permute-start.9 = (bf16[320,1024]{1,0:T(8,128)(2,1)}, bf16[320,1024]{1,0:T(8,128)(2,1)}, u32[]{:S(2)}, u32[]{:S(2)}) collective-permute-start(bf16[320,1024]{1,0:T(8,128)(2,1)} %collective-permute-done.7), channel_id=1, source_target_pairs={{0,30},{2,0},{4,2},{6,4},{8,6},{10,8},{12,10},{14,12},{16,14},{18,... | collective-permute-start | bytes 1966088 | tf_op jit(solution)/shard_map/ppermute | solution.py:21
  162.9 5.3 broadcast_in_dim.27
  174.1 16.5 %collective-permute-start.11 = (bf16[320,1024]{1,0:T(8,128)(2,1)}, bf16[320,1024]{1,0:T(8,128)(2,1)S(1)}, u32[]{:S(2)}, u32[]{:S(2)}) collective-permute-start(bf16[320,1024]{1,0:T(8,128)(2,1)} %collective-permute-done.9), channel_id=1, source_target_pairs={{0,30},{2,0},{4,2},{6,4},{8,6},{10,8},{12,10},{14,12},{16,14},{18,... | collective-permute-start | bytes 1966088 | tf_op jit(solution)/shard_map/ppermute | solution.py:21
  198.2 5.1 collective-permute-done.11
  203.3 16.5 %collective-permute-start.13 = (bf16[320,1024]{1,0:T(8,128)(2,1)S(1)}, bf16[320,1024]{1,0:T(8,128)(2,1)S(1)}, u32[]{:S(2)}, u32[]{:S(2)}) collective-permute-start(bf16[320,1024]{1,0:T(8,128)(2,1)S(1)} %collective-permute-done.11), channel_id=1, source_target_pairs={{0,30},{2,0},{4,2},{6,4},{8,6},{10,8},{12,10},{14,12},{16,14},{18,... | collective-permute-start | bytes 1966088 | tf_op jit(solution)/shard_map/ppermute | solution.py:21
  232.2 6.9 collective-permute-done.14
  240.0 16.3 %convert_bitcast_fusion = bf16[500,16,1024]{2,0,1:T(8,128)(2,1)} fusion(bf16[16,320,1024]{2,1,0:T(8,128)(2,1)} %bitcast.8, s32[16,500]{1,0:T(8,128)S(1)} %copy.35), kind=kOutput, calls=%fused_computation.22 | convolution fusion | flops 5253632000 | bytes 26901760 | tf_op jit(solution)/shard_map/scr,srd->scd/dot_general | solution.py:51
  256.3 15.5 %copy.36 = bf16[500,16,1024]{2,1,0:T(8,128)(2,1)} copy(bf16[500,16,1024]{2,0,1:T(8,128)(2,1)} %convert_bitcast_fusion) | data formatting | bytes 32768000 | tf_op jit(solution)/shard_map/convert_element_type | solution.py:56
  271.8 150.1 %while.25 = (s32[]{:T(128)}, f32[10,32,1024]{2,1,0:T(8,128)}, f32[10,32,25]{2,1,0:T(8,128)}, bf16[10,800,1024]{2,1,0:T(8,128)(2,1)}, bf16[1024,1024]{1,0:T(8,128)(2,1)}, /*index=5*/f32[1024]{0:T(1024)S(1)}, s32[]{:T(128)}) while((s32[]{:T(128)}, f32[10,32,1024]{2,1,0:T(8,128)}, f32[10,32,25]{2,1,0:T(8,128)}, bf16[10,800,1024]{2,1,0:T(8,128)(2,1)}, ...), condition=%wide.region_1.2_spmd, body=%wide.region_0.1_spmd.sunk | while | flops 1689190400 | bytes 17250768 | solution.py:76
  271.8 5.7 add_maximum_fusion.3
  281.9 4.3 fusion.56
  286.9 5.7 add_maximum_fusion.3
  296.9 4.3 fusion.56
  301.9 5.7 add_maximum_fusion.3
  311.9 4.3 fusion.56
  316.9 5.7 add_maximum_fusion.3
  331.9 5.7 add_maximum_fusion.3
  341.9 4.3 fusion.56
  346.9 5.7 add_maximum_fusion.3
  357.0 4.3 fusion.56
  361.9 5.7 add_maximum_fusion.3
  372.0 4.3 fusion.56
  376.9 5.7 add_maximum_fusion.3
  387.0 4.3 fusion.56
  392.0 5.7 add_maximum_fusion.3
  402.0 4.3 fusion.56
  407.0 5.7 add_maximum_fusion.3
  424.5 22.8 %all-reduce.8.cloned.1.call-done = f32[320,1024]{1,0:T(8,128)} async-done(((f32[320,1024]{1,0:T(8,128)}), f32[320,1024]{1,0:T(8,128)}) %all-reduce.8.cloned.1.call-update) | async-done | bytes 1310736 | tf_op jit(solution)/shard_map/psum | solution.py:79
  451.2 21.0 %all-reduce.10.cloned.1.call-done = f32[320,1024]{1,0:T(8,128)} async-done(((f32[320,1024]{1,0:T(8,128)}), f32[320,1024]{1,0:T(8,128)}) %all-reduce.10.cloned.1.call-update) | async-done | bytes 1310736 | tf_op jit(solution)/shard_map/psum | solution.py:83
  481.2 6.8 all-to-all-start
  488.0 12.8 all-reduce.12.cloned.1.call-done
  502.3 239.7 %while.26 = (s32[]{:T(128)}, f32[1024,1024]{1,0:T(8,128)}, f32[1024]{0:T(1024)S(1)}, bf16[10,800,1024]{2,1,0:T(8,128)(2,1)}, bf16[10,800,1024]{2,1,0:T(8,128)(2,...) while((s32[]{:T(128)}, f32[1024,1024]{1,0:T(8,128)}, ...), condition=%wide.region_11.12_spmd.clone, body=%wide.region_9.11_spmd.clone.sunk | while | flops 5041816576 | bytes 50894132 | solution.py:128
  509.4 5.2 convert_reduce_fusion.3
  518.9 6.3 select_add_fusion.4
  532.2 5.2 convert_reduce_fusion.3
  541.6 7.6 select_add_fusion.4
  556.2 5.2 convert_reduce_fusion.3
  565.7 7.6 select_add_fusion.4
  580.3 5.2 convert_reduce_fusion.3
  589.9 7.6 select_add_fusion.4
  604.5 5.2 convert_reduce_fusion.3
  613.9 7.6 select_add_fusion.4
  628.5 5.2 convert_reduce_fusion.3
  638.1 7.6 select_add_fusion.4
  652.7 5.2 convert_reduce_fusion.3
  662.1 7.6 select_add_fusion.4
  676.7 5.2 convert_reduce_fusion.3
  686.3 7.6 select_add_fusion.4
  700.9 5.2 convert_reduce_fusion.3
  710.3 7.6 select_add_fusion.4
  724.9 5.2 convert_reduce_fusion.3
  734.4 7.6 select_add_fusion.4
  742.0 15.5 %copy.43 = bf16[500,16,1024]{2,0,1:T(8,128)(2,1)} copy(bf16[500,16,1024]{2,1,0:T(8,128)(2,1)} %bitcast.14) | data formatting | bytes 32768000 | tf_op jit(solution)/shard_map/reshape | solution.py:131
  757.5 6.8 all-to-all-start.1
  767.8 592.5 %all-reduce.16.cloned.1.call-done = (f32[1024,1024]{1,0:T(8,128)}, f32[1024,1024]{1,0:T(8,128)}) async-done(((f32[1024,1024]{1,0:T(8,128)}, f32[1024,1024]{1,0:T(8,128)}), (f32[1024,1024]{1,0:T(8,128)}, f32[1024,1024]{1,0:T(8,128)})) %all-reduce.16.cloned.1.call-update) | async-done | bytes 8388624 | tf_op jit(solution)/shard_map/psum | solution.py:145
  1360.8 14.9 %reshape.78 = bf16[8000,1024]{1,0:T(8,128)(2,1)} reshape(bf16[16,500,1024]{2,1,0:T(8,128)(2,1)} %all-to-all-done.1) | data formatting | bytes 32768000 | tf_op jit(solution)/shard_map/reshape | solution.py:138
  1375.8 10.4 fusion.13
  1386.2 41.3 %all-reduce = (f32[1024]{0:T(1024)S(1)}, f32[1024]{0:T(1024)}) all-reduce(f32[1024]{0:T(1024)S(1)} %get-tuple-element.90, f32[1024]{0:T(1024)S(1)} %get-tuple-element.157), channel_id=1, replica_groups=mesh['nodes'=16,'stream'=2] {'nodes'}, use_global_device_ids=true, to_apply=%region_15.16 | all-reduce | flops 2048 | bytes 16384 | tf_op jit(solution)/shard_map/psum | solution.py:145
  1430.5 4.9 copy.88
  (251 shorter events, 251.3 us)
Async XLA Ops:
  7.2 441.8 %copy-start = (bf16[1024,1024]{1,0:T(8,128)(2,1)S(1)}, bf16[1024,1024]{1,0:T(8,128)(2,1)}, u32[]{:S(2)}) copy-start(bf16[1024,1024]{1,0:T(8,128)(2,1)} %param.19) | copy-start | bytes 6291460
  7.2 440.2 %all-reduce.8.cloned.1.call-start = ((), (), s32[]{:S(2)}) async-start(), calls=%async_computation.3 | async-start | bytes 2621440 | tf_op jit(solution)/shard_map/psum | solution.py:79
  7.2 31.3 %collective-permute-start = (bf16[320,1024]{1,0:T(8,128)(2,1)}, bf16[320,1024]{1,0:T(8,128)(2,1)S(1)}, u32[]{:S(2)}, u32[]{:S(2)}) collective-permute-start(bf16[320,1024]{1,0:T(8,128)(2,1)} %param.13), channel_id=1, source_target_pairs={{0,2},{2,4},{4,6},{6,8},{8,10},{10,12},{12,14},{14,16},{16,18},{18... | collective-permute-start | bytes 1966088 | tf_op jit(solution)/shard_map/ppermute | solution.py:16
  10.2 30.7 %collective-permute-start.1 = (bf16[320,1024]{1,0:T(8,128)(2,1)}, bf16[320,1024]{1,0:T(8,128)(2,1)S(1)}, u32[]{:S(2)}, u32[]{:S(2)}) collective-permute-start(bf16[320,1024]{1,0:T(8,128)(2,1)} %param.13), channel_id=1, source_target_pairs={{0,30},{2,0},{4,2},{6,4},{8,6},{10,8},{12,10},{14,12},{16,14},{18,... | collective-permute-start | bytes 1966088 | tf_op jit(solution)/shard_map/ppermute | solution.py:21
  38.6 5.6 copy-start.12
  38.6 29.5 %collective-permute-start.2 = (bf16[320,1024]{1,0:T(8,128)(2,1)S(1)}, bf16[320,1024]{1,0:T(8,128)(2,1)S(1)}, u32[]{:S(2)}, u32[]{:S(2)}) collective-permute-start(bf16[320,1024]{1,0:T(8,128)(2,1)S(1)} %collective-permute-done), channel_id=1, source_target_pairs={{0,2},{2,4},{4,6},{6,8},{8,10},{10,12},{12,14},{14,16},{16,18},{18... | collective-permute-start | bytes 1966088 | tf_op jit(solution)/shard_map/ppermute | solution.py:16
  41.0 58.4 %copy-start.8 = (bf16[320,1024]{1,0:T(8,128)(2,1)}, bf16[320,1024]{1,0:T(8,128)(2,1)S(1)}, u32[]{:S(2)}) copy-start(bf16[320,1024]{1,0:T(8,128)(2,1)S(1)} %collective-permute-done.1) | copy-start | bytes 1966084
  41.0 29.6 %collective-permute-start.3 = (bf16[320,1024]{1,0:T(8,128)(2,1)S(1)}, bf16[320,1024]{1,0:T(8,128)(2,1)S(1)}, u32[]{:S(2)}, u32[]{:S(2)}) collective-permute-start(bf16[320,1024]{1,0:T(8,128)(2,1)S(1)} %collective-permute-done.1), channel_id=1, source_target_pairs={{0,30},{2,0},{4,2},{6,4},{8,6},{10,8},{12,10},{14,12},{16,14},{18,... | collective-permute-start | bytes 1966088 | tf_op jit(solution)/shard_map/ppermute | solution.py:21
  68.1 28.7 %collective-permute-start.4 = (bf16[320,1024]{1,0:T(8,128)(2,1)S(1)}, bf16[320,1024]{1,0:T(8,128)(2,1)S(1)}, u32[]{:S(2)}, u32[]{:S(2)}) collective-permute-start(bf16[320,1024]{1,0:T(8,128)(2,1)S(1)} %collective-permute-done.2), channel_id=1, source_target_pairs={{0,2},{2,4},{4,6},{6,8},{8,10},{10,12},{12,14},{14,16},{16,18},{18... | collective-permute-start | bytes 1966088 | tf_op jit(solution)/shard_map/ppermute | solution.py:16
  70.6 26.2 %copy-start.6 = (bf16[320,1024]{1,0:T(8,128)(2,1)}, bf16[320,1024]{1,0:T(8,128)(2,1)S(1)}, u32[]{:S(2)}) copy-start(bf16[320,1024]{1,0:T(8,128)(2,1)S(1)} %collective-permute-done.3) | copy-start | bytes 1966084
  70.6 28.7 %collective-permute-start.5 = (bf16[320,1024]{1,0:T(8,128)(2,1)S(1)}, bf16[320,1024]{1,0:T(8,128)(2,1)}, u32[]{:S(2)}, u32[]{:S(2)}) collective-permute-start(bf16[320,1024]{1,0:T(8,128)(2,1)S(1)} %collective-permute-done.3), channel_id=1, source_target_pairs={{0,30},{2,0},{4,2},{6,4},{8,6},{10,8},{12,10},{14,12},{16,14},{18,... | collective-permute-start | bytes 1966088 | tf_op jit(solution)/shard_map/ppermute | solution.py:21
  96.8 18.5 %copy-start.10 = (bf16[320,1024]{1,0:T(8,128)(2,1)}, bf16[320,1024]{1,0:T(8,128)(2,1)S(1)}, u32[]{:S(2)}) copy-start(bf16[320,1024]{1,0:T(8,128)(2,1)S(1)} %collective-permute-done.4) | copy-start | bytes 1966084
  96.8 28.7 %collective-permute-start.6 = (bf16[320,1024]{1,0:T(8,128)(2,1)S(1)}, bf16[320,1024]{1,0:T(8,128)(2,1)}, u32[]{:S(2)}, u32[]{:S(2)}) collective-permute-start(bf16[320,1024]{1,0:T(8,128)(2,1)S(1)} %collective-permute-done.4), channel_id=1, source_target_pairs={{0,2},{2,4},{4,6},{6,8},{8,10},{10,12},{12,14},{14,16},{16,18},{18... | collective-permute-start | bytes 1966088 | tf_op jit(solution)/shard_map/ppermute | solution.py:16
  99.3 29.9 %collective-permute-start.7 = (bf16[320,1024]{1,0:T(8,128)(2,1)}, bf16[320,1024]{1,0:T(8,128)(2,1)}, u32[]{:S(2)}, u32[]{:S(2)}) collective-permute-start(bf16[320,1024]{1,0:T(8,128)(2,1)} %collective-permute-done.5), channel_id=1, source_target_pairs={{0,30},{2,0},{4,2},{6,4},{8,6},{10,8},{12,10},{14,12},{16,14},{18,... | collective-permute-start | bytes 1966088 | tf_op jit(solution)/shard_map/ppermute | solution.py:21
  125.5 34.9 %collective-permute-start.8 = (bf16[320,1024]{1,0:T(8,128)(2,1)}, bf16[320,1024]{1,0:T(8,128)(2,1)}, u32[]{:S(2)}, u32[]{:S(2)}) collective-permute-start(bf16[320,1024]{1,0:T(8,128)(2,1)} %collective-permute-done.6), channel_id=1, source_target_pairs={{0,2},{2,4},{4,6},{6,8},{8,10},{10,12},{12,14},{14,16},{16,18},{18... | collective-permute-start | bytes 1966088 | tf_op jit(solution)/shard_map/ppermute | solution.py:16
  129.3 44.8 %collective-permute-start.9 = (bf16[320,1024]{1,0:T(8,128)(2,1)}, bf16[320,1024]{1,0:T(8,128)(2,1)}, u32[]{:S(2)}, u32[]{:S(2)}) collective-permute-start(bf16[320,1024]{1,0:T(8,128)(2,1)} %collective-permute-done.7), channel_id=1, source_target_pairs={{0,30},{2,0},{4,2},{6,4},{8,6},{10,8},{12,10},{14,12},{16,14},{18,... | collective-permute-start | bytes 1966088 | tf_op jit(solution)/shard_map/ppermute | solution.py:21
  160.4 31.1 %collective-permute-start.10 = (bf16[320,1024]{1,0:T(8,128)(2,1)}, bf16[320,1024]{1,0:T(8,128)(2,1)}, u32[]{:S(2)}, u32[]{:S(2)}) collective-permute-start(bf16[320,1024]{1,0:T(8,128)(2,1)} %collective-permute-done.8), channel_id=1, source_target_pairs={{0,2},{2,4},{4,6},{6,8},{8,10},{10,12},{12,14},{14,16},{16,18},{18... | collective-permute-start | bytes 1966088 | tf_op jit(solution)/shard_map/ppermute | solution.py:16
  162.9 5.3 copy-start.3
  162.9 6.2 copy-start.13
  162.9 27.7 %copy-start.9 = (bf16[320,1024]{1,0:T(8,128)(2,1)S(1)}, bf16[320,1024]{1,0:T(8,128)(2,1)}, u32[]{:S(2)}) copy-start(bf16[320,1024]{1,0:T(8,128)(2,1)} %copy-done.8) | copy-start | bytes 1966084
  168.3 24.1 %copy-start.7 = (bf16[320,1024]{1,0:T(8,128)(2,1)S(1)}, bf16[320,1024]{1,0:T(8,128)(2,1)}, u32[]{:S(2)}) copy-start(bf16[320,1024]{1,0:T(8,128)(2,1)} %copy-done.6) | copy-start | bytes 1966084
  168.3 25.1 %copy-start.11 = (bf16[320,1024]{1,0:T(8,128)(2,1)S(1)}, bf16[320,1024]{1,0:T(8,128)(2,1)}, u32[]{:S(2)}) copy-start(bf16[320,1024]{1,0:T(8,128)(2,1)} %copy-done.10) | copy-start | bytes 1966084
  174.1 29.3 %collective-permute-start.11 = (bf16[320,1024]{1,0:T(8,128)(2,1)}, bf16[320,1024]{1,0:T(8,128)(2,1)S(1)}, u32[]{:S(2)}, u32[]{:S(2)}) collective-permute-start(bf16[320,1024]{1,0:T(8,128)(2,1)} %collective-permute-done.9), channel_id=1, source_target_pairs={{0,30},{2,0},{4,2},{6,4},{8,6},{10,8},{12,10},{14,12},{16,14},{18,... | collective-permute-start | bytes 1966088 | tf_op jit(solution)/shard_map/ppermute | solution.py:21
  191.5 30.3 %collective-permute-start.12 = (bf16[320,1024]{1,0:T(8,128)(2,1)}, bf16[320,1024]{1,0:T(8,128)(2,1)S(1)}, u32[]{:S(2)}, u32[]{:S(2)}) collective-permute-start(bf16[320,1024]{1,0:T(8,128)(2,1)} %collective-permute-done.10), channel_id=1, source_target_pairs={{0,2},{2,4},{4,6},{6,8},{8,10},{10,12},{12,14},{14,16},{16,18},{18... | collective-permute-start | bytes 1966088 | tf_op jit(solution)/shard_map/ppermute | solution.py:16
  203.3 28.0 %collective-permute-start.13 = (bf16[320,1024]{1,0:T(8,128)(2,1)S(1)}, bf16[320,1024]{1,0:T(8,128)(2,1)S(1)}, u32[]{:S(2)}, u32[]{:S(2)}) collective-permute-start(bf16[320,1024]{1,0:T(8,128)(2,1)S(1)} %collective-permute-done.11), channel_id=1, source_target_pairs={{0,30},{2,0},{4,2},{6,4},{8,6},{10,8},{12,10},{14,12},{16,14},{18,... | collective-permute-start | bytes 1966088 | tf_op jit(solution)/shard_map/ppermute | solution.py:21
  221.8 17.3 %collective-permute-start.14 = (bf16[320,1024]{1,0:T(8,128)(2,1)S(1)}, bf16[320,1024]{1,0:T(8,128)(2,1)S(1)}, u32[]{:S(2)}, u32[]{:S(2)}) collective-permute-start(bf16[320,1024]{1,0:T(8,128)(2,1)S(1)} %collective-permute-done.12), channel_id=1, source_target_pairs={{0,2},{2,4},{4,6},{6,8},{8,10},{10,12},{12,14},{14,16},{16,18},{18... | collective-permute-start | bytes 1966088 | tf_op jit(solution)/shard_map/ppermute | solution.py:16
  256.3 15.5 %copy-start.16 = (f32[1024]{0:T(1024)S(1)}, f32[1024]{0:T(1024)}, u32[]{:S(2)}) copy-start(f32[1024]{0:T(1024)} %param.18) | copy-start | bytes 12292
  422.0 50.3 %all-reduce.10.cloned.1.call-start = ((), (), s32[]{:S(2)}) async-start(), calls=%async_computation.4 | async-start | bytes 2621440 | tf_op jit(solution)/shard_map/psum | solution.py:83
  449.0 23.3 %copy-start.4 = (bf16[320,1024]{1,0:T(8,128)(2,1)S(1)}, bf16[320,1024]{1,0:T(8,128)(2,1)}, u32[]{:S(2)}) copy-start(bf16[320,1024]{1,0:T(8,128)(2,1)} %param.21) | copy-start | bytes 1966084
  449.0 23.3 %copy-start.14 = (f32[1024]{0:T(1024)S(1)}, f32[1024]{0:T(1024)}, u32[]{:S(2)}) copy-start(f32[1024]{0:T(1024)} %param.20) | copy-start | bytes 12292
  451.0 49.9 %all-reduce.12.cloned.1.call-start = ((), (), s32[]{:S(2)}) async-start(), calls=%async_computation.5 | async-start | bytes 2621440 | tf_op jit(solution)/shard_map/psum | solution.py:30
  481.2 276.3 %all-to-all-start = ((s32[16,1,500]{2,1,0:T(1,128)}), s32[16,1,500]{2,1,0:T(1,128)S(1)}, u32[]{:S(2)}, u32[]{:S(2)}) async-start(s32[16,1,500]{2,1,0:T(1,128)} %copy.37), calls=%async_computation | async-start | bytes 65536 | tf_op jit(solution)/shard_map/all_to_all | solution.py:133
  509.4 6.4 copy-start.15
  514.6 1.2 copy-start.17
  532.2 6.4 copy-start.15
  537.4 1.2 copy-start.17
  556.2 6.4 copy-start.15
  561.5 1.2 copy-start.17
  580.3 6.4 copy-start.15
  585.5 1.2 copy-start.17
  604.4 6.4 copy-start.15
  609.7 1.2 copy-start.17
  628.5 6.4 copy-start.15
  633.8 1.2 copy-start.17
  652.6 6.4 copy-start.15
  657.9 1.2 copy-start.17
  676.7 6.4 copy-start.15
  681.9 1.2 copy-start.17
  700.9 6.4 copy-start.15
  706.1 1.2 copy-start.17
  724.9 6.4 copy-start.15
  730.1 1.2 copy-start.17
  757.5 603.3 %all-to-all-start.1 = ((bf16[16,500,1024]{2,1,0:T(8,128)(2,1)}), bf16[16,500,1024]{2,1,0:T(8,128)(2,1)}, u32[]{:S(2)}, u32[]{:S(2)}) async-start(bf16[16,500,1024]{2,1,0:T(8,128)(2,1)} %bitcast.80), calls=%async_computation.1 | async-start | bytes 33030144 | tf_op jit(solution)/shard_map/all_to_all | solution.py:134
  764.4 595.9 %all-reduce.16.cloned.1.call-start = ((), (), s32[]{:S(2)}) async-start(), calls=%async_computation.8 | async-start | bytes 16777216 | tf_op jit(solution)/shard_map/psum | solution.py:145
  767.8 662.8 %all-reduce.14.cloned.1.call-start = ((), (), s32[]{:S(2)}) async-start(), calls=%async_computation.7 | async-start | bytes 8388608 | tf_op jit(solution)/shard_map/psum | solution.py:148
  1360.3 70.2 %reduce-scatter.2.cloned.1.call-start = ((), (), s32[]{:S(2)}) async-start(), calls=%async_computation.6 | async-start | bytes 1966080 | tf_op jit(solution)/shard_map/reduce_scatter | solution.py:142
  1360.8 15.0 %copy-start.5 = (f32[320,1024]{1,0:T(8,128)S(1)}, f32[320,1024]{1,0:T(8,128)}, u32[]{:S(2)}) copy-start(f32[320,1024]{1,0:T(8,128)} %get-tuple-element.169) | copy-start | bytes 3932164
  1430.5 4.9 copy-start.2
  1430.5 7.0 copy-start.1
Sparse Core Ops, SparseCore 0:
  422.1 25.1 all-reduce.7
  451.1 21.1 all-reduce.9
  479.7 21.1 all-reduce.11
  772.8 587.4 all-reduce.15
  1362.8 27.3 all-reduce.13
  1392.9 9.9 reduce-scatter.1
